TPU v7x, 32 devices: a whole 2x2x4 slice. The times are simulated.
32 devices in a mesh: row: 4 (over z), col: 4 (over x, core), layer: 2 (over y).
Axes of the slice: x: 2, y: 2, z: 4, core: 2. Of those that a mesh axis runs over, the one named last changes fastest.
Arguments:
- left_blocks: float32 [4, 2, 4, 4, 128, 128], P('row', 'layer', 'col'), may hold values from -1.2 to 1.2
- right_blocks: float32 [2, 4, 4, 8, 128, 128], P('layer', 'row', 'col'), may hold values from -1.2 to 1.2
- pair_stacks: int32 [4, 4, 2, 4, 3, 32], P('row', 'col', 'layer'), may hold values from 0 to 32, as said below
Outputs:
- product_window: float32 [4, 4, 32, 128, 128], P('row', 'col', 'layer')
Inputs may be any that keep to these rules, and one draw needn't show every extreme that they name: `pair_stacks`: entry 0 of a list holds left slots below 4, entry 1 right slots below 8, entry 2 product blocks below 32; the live triples stand first, every other slot holds (0, 0, 32); some list is live in all 32 slots.
All inputs are finite; a program needn't handle non-finite values.
Results may differ from a plain program's by a relative error of at most 0.0003.
Values sent between devices are 32-bit elements; how exact they have to be, the bound alone decides.
A program may use at most 64 MiB of HBM per device.

v0:
```python
import jax
import jax.numpy as jnp
from jax import lax
from jax.sharding import PartitionSpec as P

OUT_TILE = 32


def multiply(running, left_piece, right_piece, left_slot, right_slot, out_slot):
    first_blocks = jnp.take(left_piece, left_slot, axis=0)
    second_blocks = jnp.take(right_piece, right_slot, axis=0)
    products = jnp.einsum(
        "qxy,qyz->qxz",
        first_blocks,
        second_blocks,
        precision=lax.Precision.HIGHEST,
        preferred_element_type=jnp.float32,
    )
    return running.at[out_slot].add(products, mode="drop")


def piece_term(accumulated, left_piece, right_piece, triples):
    left_slot = triples[0]
    right_slot = triples[1]
    out_slot = triples[2]
    return multiply(accumulated, left_piece, right_piece, left_slot, right_slot, out_slot)


def body(left_blocks, right_blocks, pair_stacks):
    left_local = left_blocks[0, 0]
    right_local = right_blocks[0, :, 0]
    stacks = pair_stacks[0, 0, 0]
    block_width = left_local.shape[-1]
    initial = jnp.zeros((OUT_TILE, block_width, block_width), jnp.float32)
    right_whole = lax.all_gather(right_local, "row", axis=0, tiled=True)
    pieces = lax.all_gather(left_local, "col", axis=0, tiled=True)

    def visit(position, running):
        left_piece = lax.dynamic_index_in_dim(pieces, position, 0, keepdims=False)
        right_piece = lax.dynamic_index_in_dim(right_whole, position, 0, keepdims=False)
        triples = lax.dynamic_index_in_dim(stacks, position, 0, keepdims=False)
        return piece_term(running, left_piece, right_piece, triples)

    accumulated = lax.fori_loop(0, pieces.shape[0], visit, initial)
    reduced = lax.psum_scatter(accumulated, "layer", scatter_dimension=0, tiled=True)
    return reduced[None, None]


def solution(mesh):
    placed = (
        P("row", "layer", "col", None, None, None),
        P("layer", "row", "col", None, None, None),
        P("row", "col", "layer", None, None, None),
    )
    return jax.shard_map(
        body,
        mesh=mesh,
        in_specs=placed,
        out_specs=P("row", "col", "layer", None, None),
        check_vma=False,
    )
```

profile of v0, /device:TPU:0, one launch (start us, length us, event | category | flops | bytes accessed | tf_op | source)
XLA Modules:
  0.0 182.1 jit_solution(6074862939140767157)
XLA Ops:
  6.5 0.0 all-gather.5.cloned.1.call-start
  6.5 0.7 all-gather.5.cloned.1.call-update
  7.3 0.0 all-gather.7.cloned.1.call-start
  7.3 0.7 all-gather.7.cloned.1.call-update
  8.0 0.0 reduce-scatter.2.cloned.1.call-start
  8.1 0.7 copy.9
  8.7 19.6 %all-gather.5.cloned.1.call-done = f32[4,1,1,4,128,128]{5,4,3,2,1,0:T(8,128)} async-done(((f32[1,1,1,4,128,128]{5,4,3,2,1,0:T(8,128)}), f32[4,1,1,4,128,128]{5,4,3,2,1,0:T(8,128)}) %all-gather.5.cloned.1.call-update) | async-done | bytes 1048592 | tf_op jit(solution)/shard_map/all_gather | solution.py:36
  28.4 47.5 %all-gather.7.cloned.1.call-done = f32[4,1,1,8,128,128]{5,4,3,2,1,0:T(8,128)} async-done(((f32[1,1,1,8,128,128]{5,4,3,2,1,0:T(8,128)}), f32[4,1,1,8,128,128]{5,4,3,2,1,0:T(8,128)}) %all-gather.7.cloned.1.call-update) | async-done | bytes 2097168 | tf_op jit(solution)/shard_map/all_gather | solution.py:35
  75.9 1.6 broadcast_in_dim.43
  77.5 66.5 %while.13 = (s32[]{:T(128)}, f32[32,128,128]{2,1,0:T(8,128)}, s32[4,3,32]{2,1,0:T(4,128)S(1)}, f32[4,4,128,128]{3,2,1,0:T(8,128)}, f32[4,8,128,128]{3,2,1,0:T(8,128)}, /*index=5*/s32[]{:T(128)}) while((s32[]{:T(128)}, f32[32,128,128]{2,1,0:T(8,128)}, s32[4,3,32]{2,1,0:T(4,128)S(1)}, f32[4,4,128,128]{3,2,1,0:T(8,128)}, ...), condition=%wide.region_2.3_spmd, body=%wide.region_0.2_spmd.sunk | while | flops 806881984 | bytes 22555224 | solution.py:44
  77.6 1.0 dynamic-slice_bitcast_fusion.5
  78.5 1.1 dynamic-slice_bitcast_fusion.4
  79.6 2.0 %gather_fusion = f32[32,128,128]{2,1,0:T(8,128)} fusion(f32[8,128,128]{2,1,0:T(8,128)S(1)} %dynamic-slice_bitcast_fusion.4, s32[1024]{0:T(1024)S(1)} %get-tuple-element.158), kind=kCustom, calls=%fused_computation.1.clone.1 | custom fusion | bytes 4194432 | tf_op jit(solution)/shard_map/while/body/eval_jaxpr/jit(_take)/gather | solution.py:11
  81.6 2.0 %gather_fusion.1 = f32[32,128,128]{2,1,0:T(8,128)} fusion(f32[4,128,128]{2,1,0:T(8,128)S(1)} %dynamic-slice_bitcast_fusion.5, s32[1024]{0:T(1024)S(1)} %get-tuple-element.159), kind=kCustom, calls=%fused_computation.clone.1 | custom fusion | bytes 4194432 | tf_op jit(solution)/shard_map/while/body/eval_jaxpr/jit(_take)/gather | solution.py:10
  83.6 4.6 %fusion.17 = f32[32,128,128]{2,1,0:T(8,128)S(1)} fusion(f32[32,128,128]{2,1,0:T(8,128)} %gather_fusion, f32[32,128,128]{2,1,0:T(8,128)} %gather_fusion.1, pred[32]{0:T(512)(128)(4,1)S(1)} %get-tuple-element.160, pred[32]{0:T(512)(128)(4,1)S(1)} %get-tuple-element.161), kind=kOutput, calls=%fused_computation.3.clone.1 | convolution fusion | flops 806354944 | bytes 6291520 | tf_op jit(solution)/shard_map/while/body/eval_jaxpr/qxy,qyz->qxz/dot_general | solution.py:12
  88.2 5.9 %scatter_fusion = f32[32,128,128]{2,1,0:T(8,128)} fusion(f32[32,128,128]{2,1,0:T(8,128)} %get-tuple-element.169, s32[32]{0:T(128)S(1)} %get-tuple-element.155, f32[32,128,128]{2,1,0:T(8,128)S(1)} %fusion.17), kind=kCustom, calls=%fused_computation.2.clone.1 | custom fusion | flops 524288 | bytes 6291584 | tf_op jit(solution)/shard_map/while/body/eval_jaxpr/scatter-add | solution.py:19
  94.2 1.0 dynamic-slice_bitcast_fusion.5
  95.2 1.1 dynamic-slice_bitcast_fusion.4
  96.3 2.0 %gather_fusion = f32[32,128,128]{2,1,0:T(8,128)} fusion(f32[8,128,128]{2,1,0:T(8,128)S(1)} %dynamic-slice_bitcast_fusion.4, s32[1024]{0:T(1024)S(1)} %get-tuple-element.158), kind=kCustom, calls=%fused_computation.1.clone.1 | custom fusion | bytes 4194432 | tf_op jit(solution)/shard_map/while/body/eval_jaxpr/jit(_take)/gather | solution.py:11
  98.3 2.0 %gather_fusion.1 = f32[32,128,128]{2,1,0:T(8,128)} fusion(f32[4,128,128]{2,1,0:T(8,128)S(1)} %dynamic-slice_bitcast_fusion.5, s32[1024]{0:T(1024)S(1)} %get-tuple-element.159), kind=kCustom, calls=%fused_computation.clone.1 | custom fusion | bytes 4194432 | tf_op jit(solution)/shard_map/while/body/eval_jaxpr/jit(_take)/gather | solution.py:10
  100.3 4.6 %fusion.17 = f32[32,128,128]{2,1,0:T(8,128)S(1)} fusion(f32[32,128,128]{2,1,0:T(8,128)} %gather_fusion, f32[32,128,128]{2,1,0:T(8,128)} %gather_fusion.1, pred[32]{0:T(512)(128)(4,1)S(1)} %get-tuple-element.160, pred[32]{0:T(512)(128)(4,1)S(1)} %get-tuple-element.161), kind=kOutput, calls=%fused_computation.3.clone.1 | convolution fusion | flops 806354944 | bytes 6291520 | tf_op jit(solution)/shard_map/while/body/eval_jaxpr/qxy,qyz->qxz/dot_general | solution.py:12
  104.8 5.9 %scatter_fusion = f32[32,128,128]{2,1,0:T(8,128)} fusion(f32[32,128,128]{2,1,0:T(8,128)} %get-tuple-element.169, s32[32]{0:T(128)S(1)} %get-tuple-element.155, f32[32,128,128]{2,1,0:T(8,128)S(1)} %fusion.17), kind=kCustom, calls=%fused_computation.2.clone.1 | custom fusion | flops 524288 | bytes 6291584 | tf_op jit(solution)/shard_map/while/body/eval_jaxpr/scatter-add | solution.py:19
  110.8 1.0 dynamic-slice_bitcast_fusion.5
  111.8 1.1 dynamic-slice_bitcast_fusion.4
  112.9 2.0 %gather_fusion = f32[32,128,128]{2,1,0:T(8,128)} fusion(f32[8,128,128]{2,1,0:T(8,128)S(1)} %dynamic-slice_bitcast_fusion.4, s32[1024]{0:T(1024)S(1)} %get-tuple-element.158), kind=kCustom, calls=%fused_computation.1.clone.1 | custom fusion | bytes 4194432 | tf_op jit(solution)/shard_map/while/body/eval_jaxpr/jit(_take)/gather | solution.py:11
  114.9 2.0 %gather_fusion.1 = f32[32,128,128]{2,1,0:T(8,128)} fusion(f32[4,128,128]{2,1,0:T(8,128)S(1)} %dynamic-slice_bitcast_fusion.5, s32[1024]{0:T(1024)S(1)} %get-tuple-element.159), kind=kCustom, calls=%fused_computation.clone.1 | custom fusion | bytes 4194432 | tf_op jit(solution)/shard_map/while/body/eval_jaxpr/jit(_take)/gather | solution.py:10
  116.9 4.6 %fusion.17 = f32[32,128,128]{2,1,0:T(8,128)S(1)} fusion(f32[32,128,128]{2,1,0:T(8,128)} %gather_fusion, f32[32,128,128]{2,1,0:T(8,128)} %gather_fusion.1, pred[32]{0:T(512)(128)(4,1)S(1)} %get-tuple-element.160, pred[32]{0:T(512)(128)(4,1)S(1)} %get-tuple-element.161), kind=kOutput, calls=%fused_computation.3.clone.1 | convolution fusion | flops 806354944 | bytes 6291520 | tf_op jit(solution)/shard_map/while/body/eval_jaxpr/qxy,qyz->qxz/dot_general | solution.py:12
  121.4 5.9 %scatter_fusion = f32[32,128,128]{2,1,0:T(8,128)} fusion(f32[32,128,128]{2,1,0:T(8,128)} %get-tuple-element.169, s32[32]{0:T(128)S(1)} %get-tuple-element.155, f32[32,128,128]{2,1,0:T(8,128)S(1)} %fusion.17), kind=kCustom, calls=%fused_computation.2.clone.1 | custom fusion | flops 524288 | bytes 6291584 | tf_op jit(solution)/shard_map/while/body/eval_jaxpr/scatter-add | solution.py:19
  127.4 1.0 dynamic-slice_bitcast_fusion.5
  128.4 1.1 dynamic-slice_bitcast_fusion.4
  129.5 2.0 %gather_fusion = f32[32,128,128]{2,1,0:T(8,128)} fusion(f32[8,128,128]{2,1,0:T(8,128)S(1)} %dynamic-slice_bitcast_fusion.4, s32[1024]{0:T(1024)S(1)} %get-tuple-element.158), kind=kCustom, calls=%fused_computation.1.clone.1 | custom fusion | bytes 4194432 | tf_op jit(solution)/shard_map/while/body/eval_jaxpr/jit(_take)/gather | solution.py:11
  131.5 2.0 %gather_fusion.1 = f32[32,128,128]{2,1,0:T(8,128)} fusion(f32[4,128,128]{2,1,0:T(8,128)S(1)} %dynamic-slice_bitcast_fusion.5, s32[1024]{0:T(1024)S(1)} %get-tuple-element.159), kind=kCustom, calls=%fused_computation.clone.1 | custom fusion | bytes 4194432 | tf_op jit(solution)/shard_map/while/body/eval_jaxpr/jit(_take)/gather | solution.py:10
  133.5 4.6 %fusion.17 = f32[32,128,128]{2,1,0:T(8,128)S(1)} fusion(f32[32,128,128]{2,1,0:T(8,128)} %gather_fusion, f32[32,128,128]{2,1,0:T(8,128)} %gather_fusion.1, pred[32]{0:T(512)(128)(4,1)S(1)} %get-tuple-element.160, pred[32]{0:T(512)(128)(4,1)S(1)} %get-tuple-element.161), kind=kOutput, calls=%fused_computation.3.clone.1 | convolution fusion | flops 806354944 | bytes 6291520 | tf_op jit(solution)/shard_map/while/body/eval_jaxpr/qxy,qyz->qxz/dot_general | solution.py:12
  138.1 5.9 %scatter_fusion = f32[32,128,128]{2,1,0:T(8,128)} fusion(f32[32,128,128]{2,1,0:T(8,128)} %get-tuple-element.169, s32[32]{0:T(128)S(1)} %get-tuple-element.155, f32[32,128,128]{2,1,0:T(8,128)S(1)} %fusion.17), kind=kCustom, calls=%fused_computation.2.clone.1 | custom fusion | flops 524288 | bytes 6291584 | tf_op jit(solution)/shard_map/while/body/eval_jaxpr/scatter-add | solution.py:19
  144.0 0.0 reduce-scatter.2.cloned.1.call-update
  144.0 31.5 %reduce-scatter.2.cloned.1.call-done = f32[16,128,128]{2,1,0:T(8,128)} async-done(((f32[32,128,128]{2,1,0:T(8,128)}), f32[16,128,128]{2,1,0:T(8,128)}) %reduce-scatter.2.cloned.1.call-update) | async-done | bytes 1048592 | tf_op jit(solution)/shard_map/reduce_scatter | solution.py:45
  (16 shorter events, 0.1 us)
Async XLA Ops:
  6.5 21.8 %all-gather.5.cloned.1.call-start = ((), (), s32[]{:S(2)}) async-start(), calls=%async_computation.2 | async-start | bytes 1310720 | tf_op jit(solution)/shard_map/all_gather | solution.py:36
  7.3 68.7 %all-gather.7.cloned.1.call-start = ((), (), s32[]{:S(2)}) async-start(), calls=%async_computation.3 | async-start | bytes 2621440 | tf_op jit(solution)/shard_map/all_gather | solution.py:35
  8.0 167.5 %reduce-scatter.2.cloned.1.call-start = ((), (), s32[]{:S(2)}) async-start(), calls=%async_computation.1 | async-start | bytes 3145728 | tf_op jit(solution)/shard_map/reduce_scatter | solution.py:45
Sparse Core Ops, SparseCore 0:
  8.9 19.4 all-gather.4
  29.9 45.9 all-gather.6
  144.1 31.3 reduce-scatter.1
where the time goes:
time: 183 us; the launch traced here: 182 us
  waiting for transfers between devices  100 us (55%)
  local copies, waits for them, and re-layouts  26.5 us (14%)
  other arithmetic  23.7 us (13%)
  matrix products  18.2 us (10%)
  between operations  13.1 us (7%)
    all_gather x1, waiting for transfers between devices, body(): right_whole = lax.all_gather(right_local, 'row', axis=0, tiled=True)  47.5 us
    reduce_scatter x1, waiting for transfers between devices, body(): lax.psum_scatter(accumulated, 'layer', scatter_dimension=0, tiled=True)  31.5 us
    scatter-add x4, other arithmetic, multiply(): return running.at[out_slot].add(products, mode='drop')  23.7 us
    all_gather x1, waiting for transfers between devices, body(): pieces = lax.all_gather(left_local, 'col', axis=0, tiled=True)  19.6 us
    dot_general x4, matrix products, multiply(): jnp.einsum('qxy,qyz->qxz', first_blocks, second_blocks, precision=lax.Pre...  18.2 us
    gather x4, local copies, waits for them, and re-layouts, multiply(): first_blocks = jnp.take(left_piece, left_slot, axis=0)  8.03 us
    gather x4, local copies, waits for them, and re-layouts, multiply(): second_blocks = jnp.take(right_piece, right_slot, axis=0)  7.96 us
    squeeze x4, local copies, waits for them, and re-layouts, visit(): lax.dynamic_index_in_dim(right_whole, position, 0, keepdims=False)  4.33 us
  transfers between devices with their start and end apart: 3, of which 3 were waited for; matrix products, arithmetic and copies ran while one was open for 0% of the time, Pallas kernels for 0%

commit v1 on v0

--- a/solution.py
+++ b/solution.py
@@ -32,7 +32,26 @@
     stacks = pair_stacks[0, 0, 0]
     block_width = left_local.shape[-1]
     initial = jnp.zeros((OUT_TILE, block_width, block_width), jnp.float32)
-    right_whole = lax.all_gather(right_local, "row", axis=0, tiled=True)
+    peers, index, extent = (lax.axis_size("row"), lax.axis_index("row"), right_local.shape[0])
+    ahead = [(i, (i + 1) % peers) for i in range(peers)]
+    left = [(i, (i - 1) % peers) for i in range(peers)]
+    out = jnp.zeros(
+        (*right_local.shape[:0], peers * extent, *right_local.shape[0 + 1 :]), right_local.dtype
+    )
+    out = lax.dynamic_update_slice_in_dim(out, right_local, index * extent, axis=0)
+    from_left = from_right = right_local
+    half = peers // 2
+    for hop in range(1, half + 1):
+        from_left = lax.ppermute(from_left, "row", ahead)
+        out = lax.dynamic_update_slice_in_dim(
+            out, from_left, (index - hop) % peers * extent, axis=0
+        )
+        if hop < peers - half:
+            from_right = lax.ppermute(from_right, "row", left)
+            out = lax.dynamic_update_slice_in_dim(
+                out, from_right, (index + hop) % peers * extent, axis=0
+            )
+    right_whole = out
     pieces = lax.all_gather(left_local, "col", axis=0, tiled=True)
 
     def visit(position, running):

time: 183 us -> 159 us (0.87)
  waiting for transfers between devices: 100 us -> 63.2 us
  starting transfers between devices: 0.08 us -> 5.21 us
  local copies, waits for them, and re-layouts: 26.5 us -> 31.6 us
  other arithmetic: 23.7 us -> 25.9 us
    all_gather x1 -> x0, waiting for transfers between devices: 47.5 us -> none  [body(): right_whole = lax.all_gather(right_local, 'row', axis=0, tiled=True)]
    ppermute x0 -> x3, waiting for transfers between devices: none -> 29.7 us  [the longest x2 23.7 us: body(): from_left = lax.ppermute(from_left, 'row', ahead)]
    all_gather x1, waiting for transfers between devices: 19.6 us -> 0.01 us  [body(): pieces = lax.all_gather(left_local, 'col', axis=0, tiled=True)]
    ppermute x0 -> x3, starting transfers between devices: none -> 5.17 us  [the longest x2 3.08 us: body(): from_left = lax.ppermute(from_left, 'row', ahead)]
    dynamic_update_slice x0 -> x4, local copies, waits for them, and re-layouts: none -> 3.4 us  [the longest x2 1.71 us: body(): lax.dynamic_update_slice_in_dim(out, from_left, (index - hop) % peers * e...]
    scatter-add x4, other arithmetic: 23.7 us -> 25.8 us  [multiply(): return running.at[out_slot].add(products, mode='drop')]
  transfers between devices with their start and end apart: 3 -> 5, of which waited for: 3 -> 4; matrix products, arithmetic and copies ran while one was open for 0% -> 4% of each run, Pallas kernels for 0% -> 0%
where the time goes in v1:
time: 159 us; the launch traced here: 158 us
  waiting for transfers between devices  63.2 us (40%)
  local copies, waits for them, and re-layouts  31.6 us (20%)
  other arithmetic  25.9 us (16%)
  matrix products  18.2 us (11%)
  between operations  13.4 us (8%)
  starting transfers between devices  5.21 us (3%)
    reduce_scatter x1, waiting for transfers between devices, body(): lax.psum_scatter(accumulated, 'layer', scatter_dimension=0, tiled=True)  32.8 us
    scatter-add x4, other arithmetic, multiply(): return running.at[out_slot].add(products, mode='drop')  25.8 us
    ppermute x2, waiting for transfers between devices, body(): from_left = lax.ppermute(from_left, 'row', ahead)  23.7 us
    dot_general x4, matrix products, multiply(): jnp.einsum('qxy,qyz->qxz', first_blocks, second_blocks, precision=lax.Pre...  18.2 us
    gather x4, local copies, waits for them, and re-layouts, multiply(): second_blocks = jnp.take(right_piece, right_slot, axis=0)  8.1 us
    gather x4, local copies, waits for them, and re-layouts, multiply(): first_blocks = jnp.take(left_piece, left_slot, axis=0)  7.93 us
    ppermute x1, waiting for transfers between devices, body(): from_right = lax.ppermute(from_right, 'row', left)  5.98 us
    squeeze x4, local copies, waits for them, and re-layouts, visit(): lax.dynamic_index_in_dim(right_whole, position, 0, keepdims=False)  4.33 us
  transfers between devices with their start and end apart: 5, of which 4 were waited for; matrix products, arithmetic and copies ran while one was open for 4% of the time, Pallas kernels for 0%

profile of v1, /device:TPU:0, one launch (start us, length us, event | category | flops | bytes accessed | tf_op | source)
XLA Modules:
  0.0 157.8 jit_solution(17497803052309326212)
XLA Ops:
  6.5 0.0 copy-start
  6.5 0.0 all-gather.3.cloned.1.call-start
  6.5 0.7 all-gather.3.cloned.1.call-update
  7.3 0.0 reduce-scatter.2.cloned.1.call-start
  7.3 3.1 %collective-permute-start = (f32[1,8,128,128]{3,2,1,0:T(8,128)}, f32[1,8,128,128]{3,2,1,0:T(8,128)S(1)}, u32[]{:S(2)}, u32[]{:S(2)}) collective-permute-start(f32[1,8,128,128]{3,2,1,0:T(8,128)} %bitcast.38), channel_id=1, source_target_pairs={{0,8},{8,16},{16,24},{24,0},{1,9},{9,17},{17,25},{25,1},{2,10},{10... | collective-permute-start | bytes 1572872 | tf_op jit(solution)/shard_map/ppermute | solution.py:45
  10.4 2.1 %collective-permute-start.1 = (f32[1,8,128,128]{3,2,1,0:T(8,128)}, f32[1,8,128,128]{3,2,1,0:T(8,128)S(1)}, u32[]{:S(2)}, u32[]{:S(2)}) collective-permute-start(f32[1,8,128,128]{3,2,1,0:T(8,128)} %bitcast.39), channel_id=1, source_target_pairs={{0,24},{8,0},{16,8},{24,16},{1,25},{9,1},{17,9},{25,17},{2,26},{10... | collective-permute-start | bytes 1572872 | tf_op jit(solution)/shard_map/ppermute | solution.py:50
  12.5 12.9 %collective-permute-done = f32[1,8,128,128]{3,2,1,0:T(8,128)S(1)} collective-permute-done((f32[1,8,128,128]{3,2,1,0:T(8,128)}, f32[1,8,128,128]{3,2,1,0:T(8,128)S(1)}, u32[]{:S(2)}, u32[]{:S(2)}) %collective-permute-start) | collective-permute-done | bytes 524320 | tf_op jit(solution)/shard_map/ppermute | solution.py:45
  25.4 0.0 collective-permute-start.2
  25.4 0.7 copy.8
  26.1 1.6 %broadcast_in_dim.47 = f32[4,8,128,128]{3,2,1,0:T(8,128)} broadcast(f32[]{:T(128)} %constant.116.clone.1), dimensions={} | broadcast | bytes 2097156 | tf_op jit(solution)/shard_map/broadcast_in_dim | solution.py:38
  27.7 0.0 copy-done
  27.7 0.8 constant_dynamic-update-slice_fusion.3
  28.6 0.9 constant_dynamic-update-slice_fusion.2
  29.5 6.0 %collective-permute-done.1 = f32[1,8,128,128]{3,2,1,0:T(8,128)S(1)} collective-permute-done((f32[1,8,128,128]{3,2,1,0:T(8,128)}, f32[1,8,128,128]{3,2,1,0:T(8,128)S(1)}, u32[]{:S(2)}, u32[]{:S(2)}) %collective-permute-start.1) | collective-permute-done | bytes 524320 | tf_op jit(solution)/shard_map/ppermute | solution.py:50
  35.4 0.8 constant_dynamic-update-slice_fusion.1
  36.3 10.8 %collective-permute-done.2 = f32[1,8,128,128]{3,2,1,0:T(8,128)S(1)} collective-permute-done((f32[1,8,128,128]{3,2,1,0:T(8,128)S(1)}, f32[1,8,128,128]{3,2,1,0:T(8,128)S(1)}, u32[]{:S(2)}, u32[]{:S(2)}) %collective-permute-start.2) | collective-permute-done | bytes 524320 | tf_op jit(solution)/shard_map/ppermute | solution.py:45
  47.1 0.8 constant_dynamic-update-slice_fusion
  47.9 0.0 all-gather.3.cloned.1.call-done
  47.9 1.6 broadcast_in_dim.46
  49.4 68.6 %while.13 = (s32[]{:T(128)}, f32[32,128,128]{2,1,0:T(8,128)}, s32[4,3,32]{2,1,0:T(4,128)S(1)}, f32[4,4,128,128]{3,2,1,0:T(8,128)}, f32[4,8,128,128]{3,2,1,0:T(8,128)}, /*index=5*/s32[]{:T(128)}) while((s32[]{:T(128)}, f32[32,128,128]{2,1,0:T(8,128)}, s32[4,3,32]{2,1,0:T(4,128)S(1)}, f32[4,4,128,128]{3,2,1,0:T(8,128)}, ...), condition=%wide.region_2.3_spmd, body=%wide.region_0.2_spmd.sunk | while | flops 806881984 | bytes 22555224 | solution.py:63
  49.5 1.0 dynamic-slice_bitcast_fusion.5
  50.5 1.1 dynamic-slice_bitcast_fusion.4
  51.6 2.0 %gather_fusion = f32[32,128,128]{2,1,0:T(8,128)} fusion(f32[8,128,128]{2,1,0:T(8,128)S(1)} %dynamic-slice_bitcast_fusion.4, s32[1024]{0:T(1024)S(1)} %get-tuple-element.158), kind=kCustom, calls=%fused_computation.1.clone.1 | custom fusion | bytes 4194432 | tf_op jit(solution)/shard_map/while/body/eval_jaxpr/jit(_take)/gather | solution.py:11
  53.6 2.0 %gather_fusion.1 = f32[32,128,128]{2,1,0:T(8,128)} fusion(f32[4,128,128]{2,1,0:T(8,128)S(1)} %dynamic-slice_bitcast_fusion.5, s32[1024]{0:T(1024)S(1)} %get-tuple-element.159), kind=kCustom, calls=%fused_computation.clone.1 | custom fusion | bytes 4194432 | tf_op jit(solution)/shard_map/while/body/eval_jaxpr/jit(_take)/gather | solution.py:10
  55.6 4.6 %fusion.17 = f32[32,128,128]{2,1,0:T(8,128)S(1)} fusion(f32[32,128,128]{2,1,0:T(8,128)} %gather_fusion, f32[32,128,128]{2,1,0:T(8,128)} %gather_fusion.1, pred[32]{0:T(512)(128)(4,1)S(1)} %get-tuple-element.160, pred[32]{0:T(512)(128)(4,1)S(1)} %get-tuple-element.161), kind=kOutput, calls=%fused_computation.3.clone.1 | convolution fusion | flops 806354944 | bytes 6291520 | tf_op jit(solution)/shard_map/while/body/eval_jaxpr/qxy,qyz->qxz/dot_general | solution.py:12
  60.1 6.5 %scatter_fusion = f32[32,128,128]{2,1,0:T(8,128)} fusion(f32[32,128,128]{2,1,0:T(8,128)} %get-tuple-element.169, s32[32]{0:T(128)S(1)} %get-tuple-element.155, f32[32,128,128]{2,1,0:T(8,128)S(1)} %fusion.17), kind=kCustom, calls=%fused_computation.2.clone.1 | custom fusion | flops 524288 | bytes 6291584 | tf_op jit(solution)/shard_map/while/body/eval_jaxpr/scatter-add | solution.py:19
  66.7 1.0 dynamic-slice_bitcast_fusion.5
  67.7 1.1 dynamic-slice_bitcast_fusion.4
  68.8 2.0 %gather_fusion = f32[32,128,128]{2,1,0:T(8,128)} fusion(f32[8,128,128]{2,1,0:T(8,128)S(1)} %dynamic-slice_bitcast_fusion.4, s32[1024]{0:T(1024)S(1)} %get-tuple-element.158), kind=kCustom, calls=%fused_computation.1.clone.1 | custom fusion | bytes 4194432 | tf_op jit(solution)/shard_map/while/body/eval_jaxpr/jit(_take)/gather | solution.py:11
  70.8 2.0 %gather_fusion.1 = f32[32,128,128]{2,1,0:T(8,128)} fusion(f32[4,128,128]{2,1,0:T(8,128)S(1)} %dynamic-slice_bitcast_fusion.5, s32[1024]{0:T(1024)S(1)} %get-tuple-element.159), kind=kCustom, calls=%fused_computation.clone.1 | custom fusion | bytes 4194432 | tf_op jit(solution)/shard_map/while/body/eval_jaxpr/jit(_take)/gather | solution.py:10
  72.8 4.6 %fusion.17 = f32[32,128,128]{2,1,0:T(8,128)S(1)} fusion(f32[32,128,128]{2,1,0:T(8,128)} %gather_fusion, f32[32,128,128]{2,1,0:T(8,128)} %gather_fusion.1, pred[32]{0:T(512)(128)(4,1)S(1)} %get-tuple-element.160, pred[32]{0:T(512)(128)(4,1)S(1)} %get-tuple-element.161), kind=kOutput, calls=%fused_computation.3.clone.1 | convolution fusion | flops 806354944 | bytes 6291520 | tf_op jit(solution)/shard_map/while/body/eval_jaxpr/qxy,qyz->qxz/dot_general | solution.py:12
  77.3 6.4 %scatter_fusion = f32[32,128,128]{2,1,0:T(8,128)} fusion(f32[32,128,128]{2,1,0:T(8,128)} %get-tuple-element.169, s32[32]{0:T(128)S(1)} %get-tuple-element.155, f32[32,128,128]{2,1,0:T(8,128)S(1)} %fusion.17), kind=kCustom, calls=%fused_computation.2.clone.1 | custom fusion | flops 524288 | bytes 6291584 | tf_op jit(solution)/shard_map/while/body/eval_jaxpr/scatter-add | solution.py:19
  83.8 1.0 dynamic-slice_bitcast_fusion.5
  84.8 1.1 dynamic-slice_bitcast_fusion.4
  85.9 2.0 %gather_fusion = f32[32,128,128]{2,1,0:T(8,128)} fusion(f32[8,128,128]{2,1,0:T(8,128)S(1)} %dynamic-slice_bitcast_fusion.4, s32[1024]{0:T(1024)S(1)} %get-tuple-element.158), kind=kCustom, calls=%fused_computation.1.clone.1 | custom fusion | bytes 4194432 | tf_op jit(solution)/shard_map/while/body/eval_jaxpr/jit(_take)/gather | solution.py:11
  87.9 2.0 %gather_fusion.1 = f32[32,128,128]{2,1,0:T(8,128)} fusion(f32[4,128,128]{2,1,0:T(8,128)S(1)} %dynamic-slice_bitcast_fusion.5, s32[1024]{0:T(1024)S(1)} %get-tuple-element.159), kind=kCustom, calls=%fused_computation.clone.1 | custom fusion | bytes 4194432 | tf_op jit(solution)/shard_map/while/body/eval_jaxpr/jit(_take)/gather | solution.py:10
  89.9 4.6 %fusion.17 = f32[32,128,128]{2,1,0:T(8,128)S(1)} fusion(f32[32,128,128]{2,1,0:T(8,128)} %gather_fusion, f32[32,128,128]{2,1,0:T(8,128)} %gather_fusion.1, pred[32]{0:T(512)(128)(4,1)S(1)} %get-tuple-element.160, pred[32]{0:T(512)(128)(4,1)S(1)} %get-tuple-element.161), kind=kOutput, calls=%fused_computation.3.clone.1 | convolution fusion | flops 806354944 | bytes 6291520 | tf_op jit(solution)/shard_map/while/body/eval_jaxpr/qxy,qyz->qxz/dot_general | solution.py:12
  94.5 6.4 %scatter_fusion = f32[32,128,128]{2,1,0:T(8,128)} fusion(f32[32,128,128]{2,1,0:T(8,128)} %get-tuple-element.169, s32[32]{0:T(128)S(1)} %get-tuple-element.155, f32[32,128,128]{2,1,0:T(8,128)S(1)} %fusion.17), kind=kCustom, calls=%fused_computation.2.clone.1 | custom fusion | flops 524288 | bytes 6291584 | tf_op jit(solution)/shard_map/while/body/eval_jaxpr/scatter-add | solution.py:19
  101.0 1.0 dynamic-slice_bitcast_fusion.5
  102.0 1.1 dynamic-slice_bitcast_fusion.4
  103.1 2.0 %gather_fusion = f32[32,128,128]{2,1,0:T(8,128)} fusion(f32[8,128,128]{2,1,0:T(8,128)S(1)} %dynamic-slice_bitcast_fusion.4, s32[1024]{0:T(1024)S(1)} %get-tuple-element.158), kind=kCustom, calls=%fused_computation.1.clone.1 | custom fusion | bytes 4194432 | tf_op jit(solution)/shard_map/while/body/eval_jaxpr/jit(_take)/gather | solution.py:11
  105.1 2.0 %gather_fusion.1 = f32[32,128,128]{2,1,0:T(8,128)} fusion(f32[4,128,128]{2,1,0:T(8,128)S(1)} %dynamic-slice_bitcast_fusion.5, s32[1024]{0:T(1024)S(1)} %get-tuple-element.159), kind=kCustom, calls=%fused_computation.clone.1 | custom fusion | bytes 4194432 | tf_op jit(solution)/shard_map/while/body/eval_jaxpr/jit(_take)/gather | solution.py:10
  107.1 4.6 %fusion.17 = f32[32,128,128]{2,1,0:T(8,128)S(1)} fusion(f32[32,128,128]{2,1,0:T(8,128)} %gather_fusion, f32[32,128,128]{2,1,0:T(8,128)} %gather_fusion.1, pred[32]{0:T(512)(128)(4,1)S(1)} %get-tuple-element.160, pred[32]{0:T(512)(128)(4,1)S(1)} %get-tuple-element.161), kind=kOutput, calls=%fused_computation.3.clone.1 | convolution fusion | flops 806354944 | bytes 6291520 | tf_op jit(solution)/shard_map/while/body/eval_jaxpr/qxy,qyz->qxz/dot_general | solution.py:12
  111.6 6.4 %scatter_fusion = f32[32,128,128]{2,1,0:T(8,128)} fusion(f32[32,128,128]{2,1,0:T(8,128)} %get-tuple-element.169, s32[32]{0:T(128)S(1)} %get-tuple-element.155, f32[32,128,128]{2,1,0:T(8,128)S(1)} %fusion.17), kind=kCustom, calls=%fused_computation.2.clone.1 | custom fusion | flops 524288 | bytes 6291584 | tf_op jit(solution)/shard_map/while/body/eval_jaxpr/scatter-add | solution.py:19
  118.1 0.0 reduce-scatter.2.cloned.1.call-update
  118.1 32.8 %reduce-scatter.2.cloned.1.call-done = f32[16,128,128]{2,1,0:T(8,128)} async-done(((f32[32,128,128]{2,1,0:T(8,128)}), f32[16,128,128]{2,1,0:T(8,128)}) %reduce-scatter.2.cloned.1.call-update) | async-done | bytes 1048592 | tf_op jit(solution)/shard_map/reduce_scatter | solution.py:64
  (16 shorter events, 0.1 us)
Async XLA Ops:
  6.5 21.2 %copy-start = (f32[1,1,1,8,128,128]{5,4,3,2,1,0:T(8,128)S(1)}, f32[1,1,1,8,128,128]{5,4,3,2,1,0:T(8,128)}, u32[]{:S(2)}) copy-start(f32[1,1,1,8,128,128]{5,4,3,2,1,0:T(8,128)} %param.6) | copy-start | bytes 1572868
  6.5 41.3 %all-gather.3.cloned.1.call-start = ((), (), s32[]{:S(2)}) async-start(), calls=%async_computation.2 | async-start | bytes 1310720 | tf_op jit(solution)/shard_map/all_gather | solution.py:55
  7.3 143.7 %reduce-scatter.2.cloned.1.call-start = ((), (), s32[]{:S(2)}) async-start(), calls=%async_computation.1 | async-start | bytes 3145728 | tf_op jit(solution)/shard_map/reduce_scatter | solution.py:64
  7.3 18.1 %collective-permute-start = (f32[1,8,128,128]{3,2,1,0:T(8,128)}, f32[1,8,128,128]{3,2,1,0:T(8,128)S(1)}, u32[]{:S(2)}, u32[]{:S(2)}) collective-permute-start(f32[1,8,128,128]{3,2,1,0:T(8,128)} %bitcast.38), channel_id=1, source_target_pairs={{0,8},{8,16},{16,24},{24,0},{1,9},{9,17},{17,25},{25,1},{2,10},{10... | collective-permute-start | bytes 1572872 | tf_op jit(solution)/shard_map/ppermute | solution.py:45
  10.4 25.0 %collective-permute-start.1 = (f32[1,8,128,128]{3,2,1,0:T(8,128)}, f32[1,8,128,128]{3,2,1,0:T(8,128)S(1)}, u32[]{:S(2)}, u32[]{:S(2)}) collective-permute-start(f32[1,8,128,128]{3,2,1,0:T(8,128)} %bitcast.39), channel_id=1, source_target_pairs={{0,24},{8,0},{16,8},{24,16},{1,25},{9,1},{17,9},{25,17},{2,26},{10... | collective-permute-start | bytes 1572872 | tf_op jit(solution)/shard_map/ppermute | solution.py:50
  25.4 21.6 %collective-permute-start.2 = (f32[1,8,128,128]{3,2,1,0:T(8,128)S(1)}, f32[1,8,128,128]{3,2,1,0:T(8,128)S(1)}, u32[]{:S(2)}, u32[]{:S(2)}) collective-permute-start(f32[1,8,128,128]{3,2,1,0:T(8,128)S(1)} %collective-permute-done), channel_id=1, source_target_pairs={{0,8},{8,16},{16,24},{24,0},{1,9},{9,17},{17,25},{25,1},{2,10},{10... | collective-permute-start | bytes 1572872 | tf_op jit(solution)/shard_map/ppermute | solution.py:45
Sparse Core Ops, SparseCore 0:
  8.9 19.4 all-gather.2
  118.2 32.6 reduce-scatter.1
